TPU v7x, 512 devices: a whole 4x8x8 slice. The times are simulated.
512 devices in a mesh: shot: 16 (over x, z_lo), blk: 32 (over z_hi, y, core).
Axes of the slice: x: 4, y: 8, z: 8 (z_hi: 2, z_lo: 4; z = z_hi * 4 + z_lo), core: 2. Of those that a mesh axis runs over, the one named last changes fastest.
Arguments:
- state_before: float32 [16, 256, 64, 128], P('shot', 'blk'), may hold values from -7 to 7
- state_now: float32 [16, 256, 64, 128], P('shot', 'blk'), may hold values from -7 to 7
- adjoint_later: float32 [16, 256, 64, 128], P('shot', 'blk'), may hold values from -7 to 7
- adjoint_now: float32 [16, 256, 64, 128], P('shot', 'blk'), may hold values from -7 to 7
- courant_sq: float32 [256, 128, 128], P('blk', 'shot'), may hold values from 0.02 to 0.3
- epsilon: float32 [256, 128, 128], P('blk', 'shot'), may hold values from 0.02 to 0.3
- tilt_angle: float32 [256, 128, 128], P('blk', 'shot'), may hold values from 0 to 1.2
- azimuth: float32 [256, 128, 128], P('blk', 'shot'), may hold values from -3.140625 to 3.140625
- aperture_anchor: int32 [16], P('shot'), may hold values from 0 to 64, as said below
- step_index: int32 [1], replicated, may hold values from 0 to 12
- wavelet: float32 [16, 16], P('shot'), may hold values from -8 to 8
- residual_traces: float32 [16, 16, 128], P('shot'), may hold values from -6 to 6
- source_x: int32 [16], P('shot'), may hold values from 0 to 255
- source_y: int32 [16], P('shot'), may hold values from 0 to 63
- source_z: int32 [16], P('shot'), may hold values from 0 to 127
- receiver_x: int32 [16, 128], P('shot'), may hold values from 0 to 255
- receiver_y: int32 [16, 128], P('shot'), may hold values from 0 to 63
- receiver_z: int32 [16, 128], P('shot'), may hold values from 0 to 127
Outputs:
- adjoint_one: float32 [16, 256, 64, 128], P('shot', 'blk')
- adjoint_zero: float32 [16, 256, 64, 128], P('shot', 'blk')
- model_grad: float32 [256, 128, 128], P('blk', 'shot')
Inputs may be any that keep to these rules, and one draw needn't show every extreme that they name: `aperture_anchor`: each value is a multiple of 8; some shot has 0 and some shot has 64.
All inputs are finite; a program needn't handle non-finite values.
Results may differ from a plain program's by a relative error of at most 0.0003.
Values sent between devices are 32-bit elements; how exact they have to be, the bound alone decides.
A program may use at most 64 MiB of HBM per device.

v0:
```python
import jax
import jax.numpy as jnp
from jax import lax
from jax.sharding import PartitionSpec as P

STEPS = 4
COEF = (0.8, -0.2, 4.0 / 105.0, -1.0 / 280.0)


def padded_2(array, sides, width):
    for axis, dim in sides:
        size, length = (lax.axis_size(axis), array.shape[dim])
        up = [(i, (i + 1) % size) for i in range(size - 1)]
        down = [(j, i) for i, j in up]
        last = lax.slice_in_dim(array, length - width, length, axis=dim)
        leading = lax.slice_in_dim(array, 0, width, axis=dim)
        before = lax.ppermute(last, axis, up)
        after = lax.ppermute(leading, axis, down)
        array = jnp.concatenate([before, array, after], axis=dim)
    return array


def first_diff(padded, axis, count):
    summed = None
    for k in range(1, 5):
        upper_part = lax.slice_in_dim(padded, 4 + k, 4 + k + count, axis=axis)
        lower_part = lax.slice_in_dim(padded, 4 - k, 4 - k + count, axis=axis)
        addend = COEF[k - 1] * (upper_part - lower_part)
        summed = addend if summed is None else summed + addend
    return summed


def pad_axis(field, axis):
    widths = [(0, 0), (0, 0), (0, 0)]
    widths[axis] = (4, 4)
    return jnp.pad(field, widths)


def operate_shallow(field, tensor_parts):
    twice_eps, normal_x, normal_y, normal_z = tensor_parts
    rows = field.shape[0]
    extended = padded_2(field, (("blk", 0),), 4)
    slope_x = first_diff(extended, 0, rows)
    slope_y = first_diff(pad_axis(field, 1), 1, field.shape[1])
    slope_z = first_diff(pad_axis(field, 2), 2, field.shape[2])
    normal_slope = normal_x * slope_x + normal_y * slope_y + normal_z * slope_z
    flux_x = (1.0 + twice_eps) * slope_x - twice_eps * normal_x * normal_slope
    flux_y = (1.0 + twice_eps) * slope_y - twice_eps * normal_y * normal_slope
    flux_z = (1.0 + twice_eps) * slope_z - twice_eps * normal_z * normal_slope
    flux_ext = padded_2(flux_x, (("blk", 0),), 4)
    result = first_diff(flux_ext, 0, rows)
    result = result + first_diff(pad_axis(flux_y, 1), 1, field.shape[1])
    return result + first_diff(pad_axis(flux_z, 2), 2, field.shape[2])


def on_device(
    state_before,
    state_now,
    adjoint_later,
    adjoint_now,
    courant_sq,
    epsilon,
    tilt_angle,
    azimuth,
    aperture_anchor,
    step_index,
    wavelet,
    residual_traces,
    source_x,
    source_y,
    source_z,
    receiver_x,
    receiver_y,
    receiver_z,
):
    rows = state_now.shape[1]
    width_y = state_now.shape[2]
    depth = state_now.shape[3]
    block_index = lax.axis_index("blk")
    anchor = aperture_anchor[0]
    start_step = step_index[0]
    empty = jnp.zeros((rows, width_y, depth), jnp.float32)
    carried = (empty, empty, empty, empty)
    pieces = (
        lax.all_gather(courant_sq, "shot", axis=1, tiled=True),
        lax.all_gather(epsilon, "shot", axis=1, tiled=True),
        lax.all_gather(tilt_angle, "shot", axis=1, tiled=True),
        lax.all_gather(azimuth, "shot", axis=1, tiled=True),
    )
    count = pieces[0].shape[1]
    relative = jnp.int32(0) - anchor
    inside = (relative > -count) & (relative < width_y)
    offset = jnp.clip(relative + count, 0, width_y + count)
    placed = []
    for held, piece in zip(carried, pieces):
        spread = jnp.zeros((rows, width_y + 2 * count, depth), jnp.float32)
        spread = lax.dynamic_update_slice(spread, piece, (0, offset, 0))
        placed.append(jnp.where(inside, spread[:, count : count + width_y], 0.0))
    speed_term, eps_part, tilt_part, azimuth_part = tuple(placed)
    twice_eps = 2.0 * eps_part
    tensor_parts = (
        twice_eps,
        jnp.sin(tilt_part) * jnp.cos(azimuth_part),
        jnp.sin(tilt_part) * jnp.sin(azimuth_part),
        jnp.cos(tilt_part),
    )

    def operate(field):
        return operate_shallow(field, tensor_parts)

    global_x = block_index * rows + lax.broadcasted_iota(jnp.int32, (rows, width_y, depth), 0)
    cell_y = lax.broadcasted_iota(jnp.int32, (rows, width_y, depth), 1)
    cell_z = lax.broadcasted_iota(jnp.int32, (rows, width_y, depth), 2)
    source_mask = (global_x == source_x[0]) & (cell_y == source_y[0]) & (cell_z == source_z[0])
    local_rows = receiver_x[0] - block_index * rows
    plane_index = local_rows * width_y + receiver_y[0]
    receiver_inside = (local_rows >= 0) & (local_rows < rows)
    plane_pick = (
        (
            lax.broadcasted_iota(jnp.int32, (rows * width_y, plane_index.shape[0]), 0)
            == plane_index[None, :]
        )
        & receiver_inside[None, :]
    ).astype(jnp.float32)
    depth_match = (
        lax.broadcasted_iota(jnp.int32, (plane_index.shape[0], depth), 1) == receiver_z[0][:, None]
    ).astype(jnp.float32)
    previous = state_before[0]
    current = state_now[0]
    images = []
    for t in range(STEPS):
        image = operate(current)
        images.append(image)
        if t < STEPS - 1:
            amplitude = lax.dynamic_index_in_dim(wavelet[0], start_step + t, keepdims=False)
            following = 2.0 * current - previous + speed_term * image
            following = following + jnp.where(source_mask, amplitude, 0.0)
            previous, current = (current, following)
    later = adjoint_later[0]
    present = adjoint_now[0]
    shot_grad = jnp.zeros((rows, width_y, depth), jnp.float32)
    for t in reversed(range(STEPS)):
        shot_grad = shot_grad + present * images[t]
        earlier = 2.0 * present - later + operate(speed_term * present)
        samples = lax.dynamic_index_in_dim(residual_traces[0], start_step + t, keepdims=False)
        depth_pick = depth_match * samples[:, None]
        injected = jnp.dot(
            plane_pick,
            depth_pick,
            precision=lax.Precision.HIGHEST,
            preferred_element_type=jnp.float32,
        )
        earlier = earlier + injected.reshape(rows, width_y, depth)
        later, present = (present, earlier)
    grad_slab = jnp.zeros((rows, 2 * width_y, depth), jnp.float32)
    grad_slab = lax.dynamic_update_slice(grad_slab, shot_grad, (0, anchor, 0))
    model_grad = lax.psum_scatter(grad_slab, "shot", scatter_dimension=1, tiled=True)
    return (later[None], present[None], model_grad)


def solution(mesh):
    in_specs = (
        P("shot", "blk", None, None),
        P("shot", "blk", None, None),
        P("shot", "blk", None, None),
        P("shot", "blk", None, None),
        P("blk", "shot", None),
        P("blk", "shot", None),
        P("blk", "shot", None),
        P("blk", "shot", None),
        P("shot"),
        P(),
        P("shot", None),
        P("shot", None, None),
        P("shot"),
        P("shot"),
        P("shot"),
        P("shot", None),
        P("shot", None),
        P("shot", None),
    )
    out_specs = (P("shot", "blk", None, None), P("shot", "blk", None, None), P("blk", "shot", None))
    return jax.shard_map(
        on_device, mesh=mesh, in_specs=in_specs, out_specs=out_specs, check_vma=False
    )
```

profile of v0, /device:TPU:56, one launch (start us, length us, event | category | flops | bytes accessed | tf_op | source)
XLA Modules:
  0.0 521.9 jit_solution(15416640213191718624)
XLA Ops:
  7.2 1.7 slice_bitcast_fusion.1
  8.9 1.9 collective-permute-start.17
  10.8 3.6 collective-permute-start.16
  15.1 51.3 %all_gather.13 = f32[8,128,128]{2,1,0:T(8,128)S(1)} all-gather(f32[8,8,128]{2,1,0:T(8,128)} %param.22), channel_id=1, replica_groups=mesh['shot'=16,'blk'=32] {'shot'}, dimensions={1}, use_global_device_ids=true | all-gather | bytes 557056 | tf_op jit(solution)/shard_map/all_gather | solution.py:85
  66.6 1.5 dynamic_update_slice.16
  68.9 1.9 collective-permute-start.1
  70.8 3.6 collective-permute-start
  74.5 43.0 %all_gather.12 = f32[8,128,128]{2,1,0:T(8,128)S(1)} all-gather(f32[8,8,128]{2,1,0:T(8,128)S(1)} %copy-done.14), channel_id=1, replica_groups=mesh['shot'=16,'blk'=32] {'shot'}, dimensions={1}, use_global_device_ids=true | all-gather | bytes 557056 | tf_op jit(solution)/shard_map/all_gather | solution.py:86
  117.5 44.4 %all_gather.14 = f32[8,128,128]{2,1,0:T(8,128)} all-gather(f32[8,8,128]{2,1,0:T(8,128)S(1)} %copy-done.15), channel_id=1, replica_groups=mesh['shot'=16,'blk'=32] {'shot'}, dimensions={1}, use_global_device_ids=true | all-gather | bytes 557056 | tf_op jit(solution)/shard_map/all_gather | solution.py:87
  161.9 43.6 %all_gather.15 = f32[8,128,128]{2,1,0:T(8,128)S(1)} all-gather(f32[8,8,128]{2,1,0:T(8,128)S(1)} %copy-done.16), channel_id=1, replica_groups=mesh['shot'=16,'blk'=32] {'shot'}, dimensions={1}, use_global_device_ids=true | all-gather | bytes 557056 | tf_op jit(solution)/shard_map/all_gather | solution.py:88
  207.5 1.4 fusion.700
  212.4 1.5 dynamic_update_slice.15
  214.0 2.8 dynamic_update_slice.17
  216.8 1.3 broadcast.105.clone.2
  218.1 3.5 dynamic_update_slice.18
  222.3 8.0 %multiply_subtract_fusion.9 = (f32[8,64,128]{2,1,0:T(8,128)S(1)}, f32[8,64,128]{2,1,0:T(8,128)S(1)}, f32[8,64,128]{2,1,0:T(8,128)S(1)}, f32[8,64,128]{2,1,0:T(8,...) fusion(f32[8,320,128]{2,1,0:T(8,128)S(1)} %dynamic_update_slice.15, ...), kind=kLoop, calls=%fused_computation.1159 | loop fusion | flops 3735552 | bytes 3145729 | tf_op jit(solution)/shard_map/sub | solution.py:49
  231.8 2.1 multiply_subtract_fusion.21
  234.2 2.1 collective-permute-start.3
  236.2 3.6 collective-permute-start.2
  239.9 16.8 %collective-permute-start.19 = (f32[4,64,128]{2,1,0:T(8,128)S(1)}, f32[4,64,128]{2,1,0:T(8,128)S(1)}, u32[]{:S(2)}, u32[]{:S(2)}) collective-permute-start(f32[4,64,128]{2,1,0:T(8,128)S(1)} %get-tuple-element.99), channel_id=1, source_target_pairs={{0,1},{1,2},{2,3},{3,4},{4,5},{5,6},{6,7},{7,8},{8,9},{9,10},{10,1... | collective-permute-start | bytes 393224 | tf_op jit(solution)/shard_map/ppermute | solution.py:17
  256.7 1.9 collective-permute-start.18
  259.4 9.7 %collective-permute-start.5 = (f32[4,64,128]{2,1,0:T(8,128)S(1)}, f32[4,64,128]{2,1,0:T(8,128)S(1)}, u32[]{:S(2)}, u32[]{:S(2)}) collective-permute-start(f32[4,64,128]{2,1,0:T(8,128)S(1)} %get-tuple-element.81), channel_id=1, source_target_pairs={{0,1},{1,2},{2,3},{3,4},{4,5},{5,6},{6,7},{7,8},{8,9},{9,10},{10,1... | collective-permute-start | bytes 393224 | tf_op jit(solution)/shard_map/ppermute | solution.py:17
  269.0 1.9 collective-permute-start.4
  272.3 7.3 %collective-permute-done.4 = f32[4,64,128]{2,1,0:T(8,128)S(1)} collective-permute-done((f32[4,64,128]{2,1,0:T(8,128)S(1)}, f32[4,64,128]{2,1,0:T(8,128)S(1)}, u32[]{:S(2)}, u32[]{:S(2)}) %collective-permute-start.4) | collective-permute-done | bytes 131104 | tf_op jit(solution)/shard_map/ppermute | solution.py:18
  279.5 2.1 multiply_subtract_fusion.18
  281.8 11.5 %collective-permute-start.7 = (f32[4,64,128]{2,1,0:T(8,128)S(1)}, f32[4,64,128]{2,1,0:T(8,128)S(1)}, u32[]{:S(2)}, u32[]{:S(2)}) collective-permute-start(f32[4,64,128]{2,1,0:T(8,128)S(1)} %get-tuple-element.79), channel_id=1, source_target_pairs={{0,1},{1,2},{2,3},{3,4},{4,5},{5,6},{6,7},{7,8},{8,9},{9,10},{10,1... | collective-permute-start | bytes 393224 | tf_op jit(solution)/shard_map/ppermute | solution.py:17
  293.2 1.9 collective-permute-start.6
  295.2 2.4 collective-permute-start.21
  297.6 3.2 collective-permute-start.20
  301.5 7.9 %collective-permute-start.9 = (f32[4,64,128]{2,1,0:T(8,128)S(1)}, f32[4,64,128]{2,1,0:T(8,128)S(1)}, u32[]{:S(2)}, u32[]{:S(2)}) collective-permute-start(f32[4,64,128]{2,1,0:T(8,128)S(1)} %get-tuple-element.77), channel_id=1, source_target_pairs={{0,1},{1,2},{2,3},{3,4},{4,5},{5,6},{6,7},{7,8},{8,9},{9,10},{10,1... | collective-permute-start | bytes 393224 | tf_op jit(solution)/shard_map/ppermute | solution.py:17
  309.4 2.1 collective-permute-start.8
  311.5 2.1 multiply_subtract_fusion.6
  313.7 6.3 %collective-permute-done.8 = f32[4,64,128]{2,1,0:T(8,128)S(1)} collective-permute-done((f32[4,64,128]{2,1,0:T(8,128)S(1)}, f32[4,64,128]{2,1,0:T(8,128)S(1)}, u32[]{:S(2)}, u32[]{:S(2)}) %collective-permute-start.8) | collective-permute-done | bytes 131104 | tf_op jit(solution)/shard_map/ppermute | solution.py:18
  319.9 2.0 multiply_subtract_fusion.15
  322.2 11.5 %collective-permute-start.23 = (f32[4,64,128]{2,1,0:T(8,128)S(1)}, f32[4,64,128]{2,1,0:T(8,128)S(1)}, u32[]{:S(2)}, u32[]{:S(2)}) collective-permute-start(f32[4,64,128]{2,1,0:T(8,128)S(1)} %get-tuple-element.95), channel_id=1, source_target_pairs={{0,1},{1,2},{2,3},{3,4},{4,5},{5,6},{6,7},{7,8},{8,9},{9,10},{10,1... | collective-permute-start | bytes 393224 | tf_op jit(solution)/shard_map/ppermute | solution.py:17
  333.7 1.9 collective-permute-start.22
  335.6 2.5 collective-permute-done.22
  338.1 1.3 select_add_fusion.1
  339.5 9.8 %collective-permute-start.25 = (f32[4,64,128]{2,1,0:T(8,128)S(1)}, f32[4,64,128]{2,1,0:T(8,128)S(1)}, u32[]{:S(2)}, u32[]{:S(2)}) collective-permute-start(f32[4,64,128]{2,1,0:T(8,128)S(1)} %get-tuple-element.93), channel_id=1, source_target_pairs={{0,1},{1,2},{2,3},{3,4},{4,5},{5,6},{6,7},{7,8},{8,9},{9,10},{10,1... | collective-permute-start | bytes 393224 | tf_op jit(solution)/shard_map/ppermute | solution.py:17
  349.3 1.9 collective-permute-start.24
  351.3 2.5 collective-permute-done.24
  353.7 2.1 multiply_subtract_fusion.3
  356.0 9.8 %collective-permute-start.27 = (f32[4,64,128]{2,1,0:T(8,128)S(1)}, f32[4,64,128]{2,1,0:T(8,128)S(1)}, u32[]{:S(2)}, u32[]{:S(2)}) collective-permute-start(f32[4,64,128]{2,1,0:T(8,128)S(1)} %get-tuple-element.91), channel_id=1, source_target_pairs={{0,1},{1,2},{2,3},{3,4},{4,5},{5,6},{6,7},{7,8},{8,9},{9,10},{10,1... | collective-permute-start | bytes 393224 | tf_op jit(solution)/shard_map/ppermute | solution.py:17
  365.8 1.9 collective-permute-start.26
  367.7 2.5 collective-permute-done.26
  370.2 1.4 select_add_fusion
  371.6 9.8 %collective-permute-start.29 = (f32[4,64,128]{2,1,0:T(8,128)S(1)}, f32[4,64,128]{2,1,0:T(8,128)S(1)}, u32[]{:S(2)}, u32[]{:S(2)}) collective-permute-start(f32[4,64,128]{2,1,0:T(8,128)S(1)} %get-tuple-element.89), channel_id=1, source_target_pairs={{0,1},{1,2},{2,3},{3,4},{4,5},{5,6},{6,7},{7,8},{8,9},{9,10},{10,1... | collective-permute-start | bytes 393224 | tf_op jit(solution)/shard_map/ppermute | solution.py:17
  381.4 1.9 collective-permute-start.28
  383.4 2.4 collective-permute-start.11
  385.8 3.2 collective-permute-start.10
  389.0 2.1 multiply_subtract_fusion
  391.2 7.9 %collective-permute-start.31 = (f32[4,64,128]{2,1,0:T(8,128)S(1)}, f32[4,64,128]{2,1,0:T(8,128)S(1)}, u32[]{:S(2)}, u32[]{:S(2)}) collective-permute-start(f32[4,64,128]{2,1,0:T(8,128)S(1)} %get-tuple-element.87), channel_id=1, source_target_pairs={{0,1},{1,2},{2,3},{3,4},{4,5},{5,6},{6,7},{7,8},{8,9},{9,10},{10,1... | collective-permute-start | bytes 393224 | tf_op jit(solution)/shard_map/ppermute | solution.py:17
  399.2 1.9 collective-permute-start.30
  401.5 8.2 %collective-permute-done.30 = f32[4,64,128]{2,1,0:T(8,128)S(1)} collective-permute-done((f32[4,64,128]{2,1,0:T(8,128)S(1)}, f32[4,64,128]{2,1,0:T(8,128)S(1)}, u32[]{:S(2)}, u32[]{:S(2)}) %collective-permute-start.30) | collective-permute-done | bytes 131104 | tf_op jit(solution)/shard_map/ppermute | solution.py:18
  409.7 2.7 fusion.198
  413.2 11.5 %collective-permute-start.13 = (f32[4,64,128]{2,1,0:T(8,128)}, f32[4,64,128]{2,1,0:T(8,128)S(1)}, u32[]{:S(2)}, u32[]{:S(2)}) collective-permute-start(f32[4,64,128]{2,1,0:T(8,128)} %get-tuple-element.73), channel_id=1, source_target_pairs={{0,1},{1,2},{2,3},{3,4},{4,5},{5,6},{6,7},{7,8},{8,9},{9,10},{10,1... | collective-permute-start | bytes 393224 | tf_op jit(solution)/shard_map/ppermute | solution.py:17
  424.6 1.9 collective-permute-start.12
  427.4 1.8 dynamic_update_slice.19
  429.4 2.9 multiply_subtract_fusion.12
  432.5 9.8 %collective-permute-start.15 = (f32[4,64,128]{2,1,0:T(8,128)S(1)}, f32[4,64,128]{2,1,0:T(8,128)S(1)}, u32[]{:S(2)}, u32[]{:S(2)}) collective-permute-start(f32[4,64,128]{2,1,0:T(8,128)S(1)} %get-tuple-element.71), channel_id=1, source_target_pairs={{0,1},{1,2},{2,3},{3,4},{4,5},{5,6},{6,7},{7,8},{8,9},{9,10},{10,1... | collective-permute-start | bytes 393224 | tf_op jit(solution)/shard_map/ppermute | solution.py:17
  442.3 1.9 collective-permute-start.14
  444.6 2.1 collective-permute-done.14
  446.7 1.3 fusion.98
  448.0 67.0 %reduce-scatter.2.cloned.1.call-done = f32[8,8,128]{2,1,0:T(8,128)} async-done(((f32[8,128,128]{2,1,0:T(8,128)}), f32[8,8,128]{2,1,0:T(8,128)}) %reduce-scatter.2.cloned.1.call-update) | async-done | bytes 32784 | tf_op jit(solution)/shard_map/reduce_scatter | solution.py:157
  (116 shorter events, 12.1 us)
Async XLA Ops:
  7.2 507.9 %reduce-scatter.2.cloned.1.call-start = ((), (), s32[]{:S(2)}) async-start(), calls=%async_computation.1 | async-start | bytes 557056 | tf_op jit(solution)/shard_map/reduce_scatter | solution.py:157
  8.9 213.4 %collective-permute-start.17 = (f32[4,64,128]{2,1,0:T(8,128)}, f32[4,64,128]{2,1,0:T(8,128)}, u32[]{:S(2)}, u32[]{:S(2)}) collective-permute-start(f32[4,64,128]{2,1,0:T(8,128)} %get-tuple-element.101), channel_id=1, source_target_pairs={{0,1},{1,2},{2,3},{3,4},{4,5},{5,6},{6,7},{7,8},{8,9},{9,10},{10,1... | collective-permute-start | bytes 393224 | tf_op jit(solution)/shard_map/ppermute | solution.py:17
  10.8 211.5 %collective-permute-start.16 = (f32[4,64,128]{2,1,0:T(8,128)}, f32[4,64,128]{2,1,0:T(8,128)}, u32[]{:S(2)}, u32[]{:S(2)}) collective-permute-start(f32[4,64,128]{2,1,0:T(8,128)} %get-tuple-element.100), channel_id=1, source_target_pairs={{1,0},{2,1},{3,2},{4,3},{5,4},{6,5},{7,6},{8,7},{9,8},{10,9},{11,1... | collective-permute-start | bytes 393224 | tf_op jit(solution)/shard_map/ppermute | solution.py:18
  66.5 1.6 copy-start.5
  66.6 7.9 %copy-start.14 = (f32[8,8,128]{2,1,0:T(8,128)S(1)}, f32[8,8,128]{2,1,0:T(8,128)}, u32[]{:S(2)}) copy-start(f32[8,8,128]{2,1,0:T(8,128)} %param.23) | copy-start | bytes 98308
  66.6 50.9 %copy-start.15 = (f32[8,8,128]{2,1,0:T(8,128)S(1)}, f32[8,8,128]{2,1,0:T(8,128)}, u32[]{:S(2)}) copy-start(f32[8,8,128]{2,1,0:T(8,128)} %param.24) | copy-start | bytes 98308
  68.1 137.4 %copy-start.2 = (f32[8,320,128]{2,1,0:T(8,128)}, f32[8,320,128]{2,1,0:T(8,128)S(1)}, u32[]{:S(2)}) copy-start(f32[8,320,128]{2,1,0:T(8,128)S(1)} %dynamic_update_slice.16) | copy-start | bytes 3932164
  68.1 93.8 %copy-start.16 = (f32[8,8,128]{2,1,0:T(8,128)S(1)}, f32[8,8,128]{2,1,0:T(8,128)}, u32[]{:S(2)}) copy-start(f32[8,8,128]{2,1,0:T(8,128)} %param.25) | copy-start | bytes 98308
  68.1 138.0 %copy-start.7 = (f32[8,64,128]{2,1,0:T(8,128)}, f32[8,64,128]{2,1,0:T(8,128)S(1)}, u32[]{:S(2)}) copy-start(f32[8,64,128]{2,1,0:T(8,128)S(1)} %bitcast_multiply_fusion) | copy-start | bytes 786436
  68.1 139.3 %copy-start.23 = (s32[1,128]{1,0:T(1,128)S(1)}, s32[1,128]{1,0:T(1,128)}, u32[]{:S(2)}) copy-start(s32[1,128]{1,0:T(1,128)} %param.33) | copy-start | bytes 1540
  68.1 139.3 %copy-start.22 = (s32[1,128]{1,0:T(1,128)S(1)}, s32[1,128]{1,0:T(1,128)}, u32[]{:S(2)}) copy-start(s32[1,128]{1,0:T(1,128)} %param.34) | copy-start | bytes 1540
  68.2 140.8 %copy-start.17 = (s32[1,128]{1,0:T(1,128)S(1)}, s32[1,128]{1,0:T(1,128)}, u32[]{:S(2)}) copy-start(s32[1,128]{1,0:T(1,128)} %param.35) | copy-start | bytes 1540
  68.9 161.6 %collective-permute-start.1 = (f32[4,64,128]{2,1,0:T(8,128)}, f32[4,64,128]{2,1,0:T(8,128)S(1)}, u32[]{:S(2)}, u32[]{:S(2)}) collective-permute-start(f32[4,64,128]{2,1,0:T(8,128)} %get-tuple-element.85), channel_id=1, source_target_pairs={{0,1},{1,2},{2,3},{3,4},{4,5},{5,6},{6,7},{7,8},{8,9},{9,10},{10,1... | collective-permute-start | bytes 393224 | tf_op jit(solution)/shard_map/ppermute | solution.py:17
  70.8 159.7 %collective-permute-start = (f32[4,64,128]{2,1,0:T(8,128)}, f32[4,64,128]{2,1,0:T(8,128)}, u32[]{:S(2)}, u32[]{:S(2)}) collective-permute-start(f32[4,64,128]{2,1,0:T(8,128)} %get-tuple-element.84), channel_id=1, source_target_pairs={{1,0},{2,1},{3,2},{4,3},{5,4},{6,5},{7,6},{8,7},{9,8},{10,9},{11,1... | collective-permute-start | bytes 393224 | tf_op jit(solution)/shard_map/ppermute | solution.py:18
  216.8 13.6 %copy-start = (f32[8,320,128]{2,1,0:T(8,128)}, f32[8,320,128]{2,1,0:T(8,128)S(1)}, u32[]{:S(2)}) copy-start(f32[8,320,128]{2,1,0:T(8,128)S(1)} %dynamic_update_slice.17) | copy-start | bytes 3932164
  216.8 4.9 copy-start.19
  230.4 1.0 copy-start.8
  230.4 1.4 copy-start.1
  233.9 24.7 %copy-start.3 = (f32[8,320,128]{2,1,0:T(8,128)S(1)}, f32[8,320,128]{2,1,0:T(8,128)}, u32[]{:S(2)}) copy-start(f32[8,320,128]{2,1,0:T(8,128)} %copy-done.2) | copy-start | bytes 3932164
  234.0 24.7 %copy-start.6 = (f32[1,8,64,128]{3,2,1,0:T(8,128)S(1)}, f32[1,8,64,128]{3,2,1,0:T(8,128)}, u32[]{:S(2)}) copy-start(f32[1,8,64,128]{3,2,1,0:T(8,128)} %param.21) | copy-start | bytes 786436
  234.0 24.7 %copy-start.11 = (f32[512,128]{1,0:T(8,128)S(1)}, f32[512,128]{1,0:T(8,128)}, u32[]{:S(2)}) copy-start(f32[512,128]{1,0:T(8,128)} %fusion.663) | copy-start | bytes 786436
  234.0 24.7 %copy-start.13 = (f32[1,8,64,128]{3,2,1,0:T(8,128)S(1)}, f32[1,8,64,128]{3,2,1,0:T(8,128)}, u32[]{:S(2)}) copy-start(f32[1,8,64,128]{3,2,1,0:T(8,128)} %param.20) | copy-start | bytes 786436
  234.2 24.5 %collective-permute-start.3 = (f32[4,64,128]{2,1,0:T(8,128)S(1)}, f32[4,64,128]{2,1,0:T(8,128)S(1)}, u32[]{:S(2)}, u32[]{:S(2)}) collective-permute-start(f32[4,64,128]{2,1,0:T(8,128)S(1)} %get-tuple-element.83), channel_id=1, source_target_pairs={{0,1},{1,2},{2,3},{3,4},{4,5},{5,6},{6,7},{7,8},{8,9},{9,10},{10,1... | collective-permute-start | bytes 393224 | tf_op jit(solution)/shard_map/ppermute | solution.py:17
  236.2 22.4 %collective-permute-start.2 = (f32[4,64,128]{2,1,0:T(8,128)S(1)}, f32[4,64,128]{2,1,0:T(8,128)S(1)}, u32[]{:S(2)}, u32[]{:S(2)}) collective-permute-start(f32[4,64,128]{2,1,0:T(8,128)S(1)} %get-tuple-element.82), channel_id=1, source_target_pairs={{1,0},{2,1},{3,2},{4,3},{5,4},{6,5},{7,6},{8,7},{9,8},{10,9},{11,1... | collective-permute-start | bytes 393224 | tf_op jit(solution)/shard_map/ppermute | solution.py:18
  239.9 31.1 %collective-permute-start.19 = (f32[4,64,128]{2,1,0:T(8,128)S(1)}, f32[4,64,128]{2,1,0:T(8,128)S(1)}, u32[]{:S(2)}, u32[]{:S(2)}) collective-permute-start(f32[4,64,128]{2,1,0:T(8,128)S(1)} %get-tuple-element.99), channel_id=1, source_target_pairs={{0,1},{1,2},{2,3},{3,4},{4,5},{5,6},{6,7},{7,8},{8,9},{9,10},{10,1... | collective-permute-start | bytes 393224 | tf_op jit(solution)/shard_map/ppermute | solution.py:17
  256.7 14.3 %collective-permute-start.18 = (f32[4,64,128]{2,1,0:T(8,128)S(1)}, f32[4,64,128]{2,1,0:T(8,128)S(1)}, u32[]{:S(2)}, u32[]{:S(2)}) collective-permute-start(f32[4,64,128]{2,1,0:T(8,128)S(1)} %get-tuple-element.98), channel_id=1, source_target_pairs={{1,0},{2,1},{3,2},{4,3},{5,4},{6,5},{7,6},{8,7},{9,8},{10,9},{11,1... | collective-permute-start | bytes 393224 | tf_op jit(solution)/shard_map/ppermute | solution.py:18
  258.7 12.3 %copy-start.4 = (f32[1,8,64,128]{3,2,1,0:T(8,128)S(1)}, f32[1,8,64,128]{3,2,1,0:T(8,128)}, u32[]{:S(2)}) copy-start(f32[1,8,64,128]{3,2,1,0:T(8,128)} %param.19) | copy-start | bytes 786436
  258.7 12.3 %copy-start.12 = (f32[1,8,64,128]{3,2,1,0:T(8,128)S(1)}, f32[1,8,64,128]{3,2,1,0:T(8,128)}, u32[]{:S(2)}) copy-start(f32[1,8,64,128]{3,2,1,0:T(8,128)} %param.18) | copy-start | bytes 786436
  258.7 12.3 %copy-start.18 = (pred[64]{0:T(512)(128)(4,1)S(1)}, pred[64]{0:T(512)(128)(4,1)}, u32[]{:S(2)}) copy-start(pred[64]{0:T(512)(128)(4,1)} %iota_compare_fusion.7) | copy-start | bytes 196
  259.4 12.9 %collective-permute-start.5 = (f32[4,64,128]{2,1,0:T(8,128)S(1)}, f32[4,64,128]{2,1,0:T(8,128)S(1)}, u32[]{:S(2)}, u32[]{:S(2)}) collective-permute-start(f32[4,64,128]{2,1,0:T(8,128)S(1)} %get-tuple-element.81), channel_id=1, source_target_pairs={{0,1},{1,2},{2,3},{3,4},{4,5},{5,6},{6,7},{7,8},{8,9},{9,10},{10,1... | collective-permute-start | bytes 393224 | tf_op jit(solution)/shard_map/ppermute | solution.py:17
  269.0 10.5 %collective-permute-start.4 = (f32[4,64,128]{2,1,0:T(8,128)S(1)}, f32[4,64,128]{2,1,0:T(8,128)S(1)}, u32[]{:S(2)}, u32[]{:S(2)}) collective-permute-start(f32[4,64,128]{2,1,0:T(8,128)S(1)} %get-tuple-element.80), channel_id=1, source_target_pairs={{1,0},{2,1},{3,2},{4,3},{5,4},{6,5},{7,6},{8,7},{9,8},{10,9},{11,1... | collective-permute-start | bytes 393224 | tf_op jit(solution)/shard_map/ppermute | solution.py:18
  281.6 19.2 %copy-start.10 = (f32[512,128]{1,0:T(8,128)S(1)}, f32[512,128]{1,0:T(8,128)}, u32[]{:S(2)}) copy-start(f32[512,128]{1,0:T(8,128)} %fusion.661) | copy-start | bytes 786436
  281.8 19.0 %collective-permute-start.7 = (f32[4,64,128]{2,1,0:T(8,128)S(1)}, f32[4,64,128]{2,1,0:T(8,128)S(1)}, u32[]{:S(2)}, u32[]{:S(2)}) collective-permute-start(f32[4,64,128]{2,1,0:T(8,128)S(1)} %get-tuple-element.79), channel_id=1, source_target_pairs={{0,1},{1,2},{2,3},{3,4},{4,5},{5,6},{6,7},{7,8},{8,9},{9,10},{10,1... | collective-permute-start | bytes 393224 | tf_op jit(solution)/shard_map/ppermute | solution.py:17
  293.2 7.5 %collective-permute-start.6 = (f32[4,64,128]{2,1,0:T(8,128)S(1)}, f32[4,64,128]{2,1,0:T(8,128)S(1)}, u32[]{:S(2)}, u32[]{:S(2)}) collective-permute-start(f32[4,64,128]{2,1,0:T(8,128)S(1)} %get-tuple-element.78), channel_id=1, source_target_pairs={{1,0},{2,1},{3,2},{4,3},{5,4},{6,5},{7,6},{8,7},{9,8},{10,9},{11,1... | collective-permute-start | bytes 393224 | tf_op jit(solution)/shard_map/ppermute | solution.py:18
  295.2 16.3 %collective-permute-start.21 = (f32[4,64,128]{2,1,0:T(8,128)S(1)}, f32[4,64,128]{2,1,0:T(8,128)S(1)}, u32[]{:S(2)}, u32[]{:S(2)}) collective-permute-start(f32[4,64,128]{2,1,0:T(8,128)S(1)} %get-tuple-element.97), channel_id=1, source_target_pairs={{0,1},{1,2},{2,3},{3,4},{4,5},{5,6},{6,7},{7,8},{8,9},{9,10},{10,1... | collective-permute-start | bytes 393224 | tf_op jit(solution)/shard_map/ppermute | solution.py:17
  297.6 13.9 %collective-permute-start.20 = (f32[4,64,128]{2,1,0:T(8,128)S(1)}, f32[4,64,128]{2,1,0:T(8,128)S(1)}, u32[]{:S(2)}, u32[]{:S(2)}) collective-permute-start(f32[4,64,128]{2,1,0:T(8,128)S(1)} %get-tuple-element.96), channel_id=1, source_target_pairs={{1,0},{2,1},{3,2},{4,3},{5,4},{6,5},{7,6},{8,7},{9,8},{10,9},{11,1... | collective-permute-start | bytes 393224 | tf_op jit(solution)/shard_map/ppermute | solution.py:18
  301.5 12.2 %collective-permute-start.9 = (f32[4,64,128]{2,1,0:T(8,128)S(1)}, f32[4,64,128]{2,1,0:T(8,128)S(1)}, u32[]{:S(2)}, u32[]{:S(2)}) collective-permute-start(f32[4,64,128]{2,1,0:T(8,128)S(1)} %get-tuple-element.77), channel_id=1, source_target_pairs={{0,1},{1,2},{2,3},{3,4},{4,5},{5,6},{6,7},{7,8},{8,9},{9,10},{10,1... | collective-permute-start | bytes 393224 | tf_op jit(solution)/shard_map/ppermute | solution.py:17
  309.4 10.5 %collective-permute-start.8 = (f32[4,64,128]{2,1,0:T(8,128)S(1)}, f32[4,64,128]{2,1,0:T(8,128)S(1)}, u32[]{:S(2)}, u32[]{:S(2)}) collective-permute-start(f32[4,64,128]{2,1,0:T(8,128)S(1)} %get-tuple-element.76), channel_id=1, source_target_pairs={{1,0},{2,1},{3,2},{4,3},{5,4},{6,5},{7,6},{8,7},{9,8},{10,9},{11,1... | collective-permute-start | bytes 393224 | tf_op jit(solution)/shard_map/ppermute | solution.py:18
  322.2 13.4 %collective-permute-start.23 = (f32[4,64,128]{2,1,0:T(8,128)S(1)}, f32[4,64,128]{2,1,0:T(8,128)S(1)}, u32[]{:S(2)}, u32[]{:S(2)}) collective-permute-start(f32[4,64,128]{2,1,0:T(8,128)S(1)} %get-tuple-element.95), channel_id=1, source_target_pairs={{0,1},{1,2},{2,3},{3,4},{4,5},{5,6},{6,7},{7,8},{8,9},{9,10},{10,1... | collective-permute-start | bytes 393224 | tf_op jit(solution)/shard_map/ppermute | solution.py:17
  333.7 4.4 collective-permute-start.22
  339.5 11.7 %collective-permute-start.25 = (f32[4,64,128]{2,1,0:T(8,128)S(1)}, f32[4,64,128]{2,1,0:T(8,128)S(1)}, u32[]{:S(2)}, u32[]{:S(2)}) collective-permute-start(f32[4,64,128]{2,1,0:T(8,128)S(1)} %get-tuple-element.93), channel_id=1, source_target_pairs={{0,1},{1,2},{2,3},{3,4},{4,5},{5,6},{6,7},{7,8},{8,9},{9,10},{10,1... | collective-permute-start | bytes 393224 | tf_op jit(solution)/shard_map/ppermute | solution.py:17
  349.3 4.4 collective-permute-start.24
  356.0 11.7 %collective-permute-start.27 = (f32[4,64,128]{2,1,0:T(8,128)S(1)}, f32[4,64,128]{2,1,0:T(8,128)S(1)}, u32[]{:S(2)}, u32[]{:S(2)}) collective-permute-start(f32[4,64,128]{2,1,0:T(8,128)S(1)} %get-tuple-element.91), channel_id=1, source_target_pairs={{0,1},{1,2},{2,3},{3,4},{4,5},{5,6},{6,7},{7,8},{8,9},{9,10},{10,1... | collective-permute-start | bytes 393224 | tf_op jit(solution)/shard_map/ppermute | solution.py:17
  365.8 4.4 collective-permute-start.26
  371.6 17.3 %collective-permute-start.29 = (f32[4,64,128]{2,1,0:T(8,128)S(1)}, f32[4,64,128]{2,1,0:T(8,128)S(1)}, u32[]{:S(2)}, u32[]{:S(2)}) collective-permute-start(f32[4,64,128]{2,1,0:T(8,128)S(1)} %get-tuple-element.89), channel_id=1, source_target_pairs={{0,1},{1,2},{2,3},{3,4},{4,5},{5,6},{6,7},{7,8},{8,9},{9,10},{10,1... | collective-permute-start | bytes 393224 | tf_op jit(solution)/shard_map/ppermute | solution.py:17
  381.4 7.5 %collective-permute-start.28 = (f32[4,64,128]{2,1,0:T(8,128)S(1)}, f32[4,64,128]{2,1,0:T(8,128)S(1)}, u32[]{:S(2)}, u32[]{:S(2)}) collective-permute-start(f32[4,64,128]{2,1,0:T(8,128)S(1)} %get-tuple-element.88), channel_id=1, source_target_pairs={{1,0},{2,1},{3,2},{4,3},{5,4},{6,5},{7,6},{8,7},{9,8},{10,9},{11,1... | collective-permute-start | bytes 393224 | tf_op jit(solution)/shard_map/ppermute | solution.py:18
  383.4 18.1 %collective-permute-start.11 = (f32[4,64,128]{2,1,0:T(8,128)S(1)}, f32[4,64,128]{2,1,0:T(8,128)S(1)}, u32[]{:S(2)}, u32[]{:S(2)}) collective-permute-start(f32[4,64,128]{2,1,0:T(8,128)S(1)} %get-tuple-element.75), channel_id=1, source_target_pairs={{0,1},{1,2},{2,3},{3,4},{4,5},{5,6},{6,7},{7,8},{8,9},{9,10},{10,1... | collective-permute-start | bytes 393224 | tf_op jit(solution)/shard_map/ppermute | solution.py:17
  385.8 15.7 %collective-permute-start.10 = (f32[4,64,128]{2,1,0:T(8,128)S(1)}, f32[4,64,128]{2,1,0:T(8,128)S(1)}, u32[]{:S(2)}, u32[]{:S(2)}) collective-permute-start(f32[4,64,128]{2,1,0:T(8,128)S(1)} %get-tuple-element.74), channel_id=1, source_target_pairs={{1,0},{2,1},{3,2},{4,3},{5,4},{6,5},{7,6},{8,7},{9,8},{10,9},{11,1... | collective-permute-start | bytes 393224 | tf_op jit(solution)/shard_map/ppermute | solution.py:18
  391.0 10.1 %copy-start.21 = (f32[128]{0:T(128)S(1)}, f32[128]{0:T(128)}, u32[]{:S(2)}) copy-start(f32[128]{0:T(128)} %get-tuple-element.105) | copy-start | bytes 1540
  391.2 10.3 %collective-permute-start.31 = (f32[4,64,128]{2,1,0:T(8,128)S(1)}, f32[4,64,128]{2,1,0:T(8,128)S(1)}, u32[]{:S(2)}, u32[]{:S(2)}) collective-permute-start(f32[4,64,128]{2,1,0:T(8,128)S(1)} %get-tuple-element.87), channel_id=1, source_target_pairs={{0,1},{1,2},{2,3},{3,4},{4,5},{5,6},{6,7},{7,8},{8,9},{9,10},{10,1... | collective-permute-start | bytes 393224 | tf_op jit(solution)/shard_map/ppermute | solution.py:17
  399.2 10.5 %collective-permute-start.30 = (f32[4,64,128]{2,1,0:T(8,128)S(1)}, f32[4,64,128]{2,1,0:T(8,128)S(1)}, u32[]{:S(2)}, u32[]{:S(2)}) collective-permute-start(f32[4,64,128]{2,1,0:T(8,128)S(1)} %get-tuple-element.86), channel_id=1, source_target_pairs={{1,0},{2,1},{3,2},{4,3},{5,4},{6,5},{7,6},{8,7},{9,8},{10,9},{11,1... | collective-permute-start | bytes 393224 | tf_op jit(solution)/shard_map/ppermute | solution.py:18
  412.4 34.3 %copy-start.9 = (f32[8,64,128]{2,1,0:T(8,128)}, f32[8,64,128]{2,1,0:T(8,128)S(1)}, u32[]{:S(2)}) copy-start(f32[8,64,128]{2,1,0:T(8,128)S(1)} %get-tuple-element.4) | copy-start | bytes 786436
  413.2 16.1 %collective-permute-start.13 = (f32[4,64,128]{2,1,0:T(8,128)}, f32[4,64,128]{2,1,0:T(8,128)S(1)}, u32[]{:S(2)}, u32[]{:S(2)}) collective-permute-start(f32[4,64,128]{2,1,0:T(8,128)} %get-tuple-element.73), channel_id=1, source_target_pairs={{0,1},{1,2},{2,3},{3,4},{4,5},{5,6},{6,7},{7,8},{8,9},{9,10},{10,1... | collective-permute-start | bytes 393224 | tf_op jit(solution)/shard_map/ppermute | solution.py:17
  424.6 4.7 collective-permute-start.12
  432.3 11.9 %copy-start.20 = (f32[128]{0:T(128)S(1)}, f32[128]{0:T(128)}, u32[]{:S(2)}) copy-start(f32[128]{0:T(128)} %get-tuple-element.102) | copy-start | bytes 1540
  432.5 12.1 %collective-permute-start.15 = (f32[4,64,128]{2,1,0:T(8,128)S(1)}, f32[4,64,128]{2,1,0:T(8,128)S(1)}, u32[]{:S(2)}, u32[]{:S(2)}) collective-permute-start(f32[4,64,128]{2,1,0:T(8,128)S(1)} %get-tuple-element.71), channel_id=1, source_target_pairs={{0,1},{1,2},{2,3},{3,4},{4,5},{5,6},{6,7},{7,8},{8,9},{9,10},{10,1... | collective-permute-start | bytes 393224 | tf_op jit(solution)/shard_map/ppermute | solution.py:17
  442.3 4.4 collective-permute-start.14
Sparse Core Ops, SparseCore 0:
  429.4 85.6 reduce-scatter.1
where the time goes:
time: 523 us; the launch traced here: 522 us
  blocking collectives  182 us (35%)
  starting transfers between devices  165 us (32%)
  waiting for transfers between devices  98.5 us (19%)
  other arithmetic  34.3 us (7%)
  local copies, waits for them, and re-layouts  20.4 us (4%)
  between operations  18.4 us (4%)
    ppermute x16, starting transfers between devices, padded_2(): before = lax.ppermute(last, axis, up)  127 us
    reduce_scatter x1, waiting for transfers between devices, on_device(): lax.psum_scatter(grad_slab, 'shot', scatter_dimension=1, tiled=True)  67 us
    all_gather x1, blocking collectives, on_device(): lax.all_gather(courant_sq, 'shot', axis=1, tiled=True)  51.3 us
    all_gather x1, blocking collectives, on_device(): lax.all_gather(tilt_angle, 'shot', axis=1, tiled=True)  44.4 us
    all_gather x1, blocking collectives, on_device(): lax.all_gather(azimuth, 'shot', axis=1, tiled=True)  43.6 us
    all_gather x1, blocking collectives, on_device(): lax.all_gather(epsilon, 'shot', axis=1, tiled=True)  43 us
    ppermute x16, starting transfers between devices, padded_2(): after = lax.ppermute(leading, axis, down)  38.5 us
    ppermute x16, waiting for transfers between devices, padded_2(): after = lax.ppermute(leading, axis, down)  31.4 us
  transfers between devices with their start and end apart: 33, of which 9 were waited for; matrix products, arithmetic and copies ran while one was open for 8% of the time, Pallas kernels for 0%

commit v1 on v0

--- a/solution.py
+++ b/solution.py
@@ -5,6 +5,13 @@
 
 STEPS = 4
 COEF = (0.8, -0.2, 4.0 / 105.0, -1.0 / 280.0)
+
+
+def gather_over(array, axis, along):
+    peers = lax.axis_size(axis)
+    pieces = jnp.stack([array for _ in range(peers)])
+    pieces = lax.all_to_all(pieces, axis, split_axis=0, concat_axis=0)
+    return jnp.concatenate(pieces, axis=along)
 
 
 def padded_2(array, sides, width):
@@ -84,7 +91,7 @@
     pieces = (
         lax.all_gather(courant_sq, "shot", axis=1, tiled=True),
         lax.all_gather(epsilon, "shot", axis=1, tiled=True),
-        lax.all_gather(tilt_angle, "shot", axis=1, tiled=True),
+        gather_over(tilt_angle, "shot", 1),
         lax.all_gather(azimuth, "shot", axis=1, tiled=True),
     )
     count = pieces[0].shape[1]

time: 523 us -> 488 us (0.933)
  blocking collectives: 182 us -> 136 us
  starting transfers between devices: 165 us -> 176 us
    all_gather x1 -> x0, blocking collectives: 44.4 us -> none  [on_device(): lax.all_gather(tilt_angle, 'shot', axis=1, tiled=True)]
    all_to_all x0 -> x1, starting transfers between devices: none -> 9.83 us  [gather_over(): pieces = lax.all_to_all(pieces, axis, split_axis=0, concat_axis=0)]
  transfers between devices with their start and end apart: 33 -> 34, of which waited for: 9 -> 9; matrix products, arithmetic and copies ran while one was open for 8% -> 8% of each run, Pallas kernels for 0% -> 0%
where the time goes in v1:
time: 488 us; the launch traced here: 487 us
  starting transfers between devices  176 us (36%)
  blocking collectives  136 us (28%)
  waiting for transfers between devices  98.5 us (20%)
  other arithmetic  30.4 us (6%)
  local copies, waits for them, and re-layouts  24 us (5%)
  between operations  18.4 us (4%)
    ppermute x16, starting transfers between devices, padded_2(): before = lax.ppermute(last, axis, up)  128 us
    reduce_scatter x1, waiting for transfers between devices, on_device(): lax.psum_scatter(grad_slab, 'shot', scatter_dimension=1, tiled=True)  67 us
    all_gather x1, blocking collectives, on_device(): lax.all_gather(courant_sq, 'shot', axis=1, tiled=True)  49.3 us
    all_gather x1, blocking collectives, on_device(): lax.all_gather(epsilon, 'shot', axis=1, tiled=True)  44.2 us
    all_gather x1, blocking collectives, on_device(): lax.all_gather(azimuth, 'shot', axis=1, tiled=True)  42.8 us
    ppermute x16, starting transfers between devices, padded_2(): after = lax.ppermute(leading, axis, down)  38.5 us
    ppermute x16, waiting for transfers between devices, padded_2(): after = lax.ppermute(leading, axis, down)  31.4 us
    sub x8, other arithmetic, operate_shallow(): flux_z = (1.0 + twice_eps) * slope_z - twice_eps * normal_z * normal_slope  19.6 us
  transfers between devices with their start and end apart: 34, of which 9 were waited for; matrix products, arithmetic and copies ran while one was open for 8% of the time, Pallas kernels for 0%

profile of v1, /device:TPU:56, one launch (start us, length us, event | category | flops | bytes accessed | tf_op | source)
XLA Modules:
  0.0 486.6 jit_solution(7245020446904782055)
XLA Ops:
  7.2 1.7 stack.2
  8.8 9.8 %all-to-all-start = ((f32[16,8,8,128]{3,2,1,0:T(8,128)}), f32[16,8,8,128]{3,2,1,0:T(8,128)S(1)}, u32[]{:S(2)}, u32[]{:S(2)}) async-start(f32[16,8,8,128]{3,2,1,0:T(8,128)} %stack.2), calls=%async_computation | async-start | bytes 1048576 | tf_op jit(solution)/shard_map/all_to_all | solution.py:13
  19.5 1.9 collective-permute-start.17
  21.4 3.6 collective-permute-start.16
  25.7 49.3 %all_gather.10 = f32[8,128,128]{2,1,0:T(8,128)S(1)} all-gather(f32[8,8,128]{2,1,0:T(8,128)S(1)} %copy-done.13), channel_id=1, replica_groups=mesh['shot'=16,'blk'=32] {'shot'}, dimensions={1}, use_global_device_ids=true | all-gather | bytes 557056 | tf_op jit(solution)/shard_map/all_gather | solution.py:92
  75.1 1.5 dynamic_update_slice.16
  77.5 1.9 collective-permute-start.1
  79.4 3.6 collective-permute-start
  84.4 1.4 fusion.700
  88.6 44.2 %all_gather.9 = f32[8,128,128]{2,1,0:T(8,128)} all-gather(f32[8,8,128]{2,1,0:T(8,128)S(1)} %copy-done.14), channel_id=1, replica_groups=mesh['shot'=16,'blk'=32] {'shot'}, dimensions={1}, use_global_device_ids=true | all-gather | bytes 557056 | tf_op jit(solution)/shard_map/all_gather | solution.py:93
  132.7 42.8 %all_gather.11 = f32[8,128,128]{2,1,0:T(8,128)S(1)} all-gather(f32[8,8,128]{2,1,0:T(8,128)S(1)} %copy-done.15), channel_id=1, replica_groups=mesh['shot'=16,'blk'=32] {'shot'}, dimensions={1}, use_global_device_ids=true | all-gather | bytes 557056 | tf_op jit(solution)/shard_map/all_gather | solution.py:95
  176.9 2.8 dynamic_update_slice.15
  180.9 3.5 dynamic_update_slice.18
  186.5 2.8 dynamic_update_slice.17
  190.4 4.3 multiply_subtract_fusion.9
  196.0 2.1 multiply_subtract_fusion.21
  198.3 2.1 collective-permute-start.3
  200.4 3.6 collective-permute-start.2
  204.1 18.0 %collective-permute-start.19 = (f32[4,64,128]{2,1,0:T(8,128)S(1)}, f32[4,64,128]{2,1,0:T(8,128)S(1)}, u32[]{:S(2)}, u32[]{:S(2)}) collective-permute-start(f32[4,64,128]{2,1,0:T(8,128)S(1)} %get-tuple-element.99), channel_id=1, source_target_pairs={{0,1},{1,2},{2,3},{3,4},{4,5},{5,6},{6,7},{7,8},{8,9},{9,10},{10,1... | collective-permute-start | bytes 393224 | tf_op jit(solution)/shard_map/ppermute | solution.py:24
  222.1 1.9 collective-permute-start.18
  224.8 9.7 %collective-permute-start.5 = (f32[4,64,128]{2,1,0:T(8,128)S(1)}, f32[4,64,128]{2,1,0:T(8,128)S(1)}, u32[]{:S(2)}, u32[]{:S(2)}) collective-permute-start(f32[4,64,128]{2,1,0:T(8,128)S(1)} %get-tuple-element.81), channel_id=1, source_target_pairs={{0,1},{1,2},{2,3},{3,4},{4,5},{5,6},{6,7},{7,8},{8,9},{9,10},{10,1... | collective-permute-start | bytes 393224 | tf_op jit(solution)/shard_map/ppermute | solution.py:24
  234.4 1.9 collective-permute-start.4
  236.4 1.4 fusion.655
  237.8 7.1 %collective-permute-done.4 = f32[4,64,128]{2,1,0:T(8,128)S(1)} collective-permute-done((f32[4,64,128]{2,1,0:T(8,128)S(1)}, f32[4,64,128]{2,1,0:T(8,128)S(1)}, u32[]{:S(2)}, u32[]{:S(2)}) %collective-permute-start.4) | collective-permute-done | bytes 131104 | tf_op jit(solution)/shard_map/ppermute | solution.py:25
  244.9 2.1 multiply_subtract_fusion.18
  247.2 11.5 %collective-permute-start.7 = (f32[4,64,128]{2,1,0:T(8,128)S(1)}, f32[4,64,128]{2,1,0:T(8,128)S(1)}, u32[]{:S(2)}, u32[]{:S(2)}) collective-permute-start(f32[4,64,128]{2,1,0:T(8,128)S(1)} %get-tuple-element.79), channel_id=1, source_target_pairs={{0,1},{1,2},{2,3},{3,4},{4,5},{5,6},{6,7},{7,8},{8,9},{9,10},{10,1... | collective-permute-start | bytes 393224 | tf_op jit(solution)/shard_map/ppermute | solution.py:24
  258.6 1.9 collective-permute-start.6
  260.6 2.4 collective-permute-start.21
  263.0 3.2 collective-permute-start.20
  266.9 7.9 %collective-permute-start.9 = (f32[4,64,128]{2,1,0:T(8,128)S(1)}, f32[4,64,128]{2,1,0:T(8,128)S(1)}, u32[]{:S(2)}, u32[]{:S(2)}) collective-permute-start(f32[4,64,128]{2,1,0:T(8,128)S(1)} %get-tuple-element.77), channel_id=1, source_target_pairs={{0,1},{1,2},{2,3},{3,4},{4,5},{5,6},{6,7},{7,8},{8,9},{9,10},{10,1... | collective-permute-start | bytes 393224 | tf_op jit(solution)/shard_map/ppermute | solution.py:24
  274.8 2.1 collective-permute-start.8
  277.0 2.1 multiply_subtract_fusion.6
  279.1 6.3 %collective-permute-done.8 = f32[4,64,128]{2,1,0:T(8,128)S(1)} collective-permute-done((f32[4,64,128]{2,1,0:T(8,128)S(1)}, f32[4,64,128]{2,1,0:T(8,128)S(1)}, u32[]{:S(2)}, u32[]{:S(2)}) %collective-permute-start.8) | collective-permute-done | bytes 131104 | tf_op jit(solution)/shard_map/ppermute | solution.py:25
  285.3 2.1 multiply_subtract_fusion.15
  287.6 11.5 %collective-permute-start.23 = (f32[4,64,128]{2,1,0:T(8,128)S(1)}, f32[4,64,128]{2,1,0:T(8,128)S(1)}, u32[]{:S(2)}, u32[]{:S(2)}) collective-permute-start(f32[4,64,128]{2,1,0:T(8,128)S(1)} %get-tuple-element.95), channel_id=1, source_target_pairs={{0,1},{1,2},{2,3},{3,4},{4,5},{5,6},{6,7},{7,8},{8,9},{9,10},{10,1... | collective-permute-start | bytes 393224 | tf_op jit(solution)/shard_map/ppermute | solution.py:24
  299.1 1.9 collective-permute-start.22
  301.1 2.5 collective-permute-done.22
  303.5 1.2 select_add_fusion.1
  304.8 9.8 %collective-permute-start.25 = (f32[4,64,128]{2,1,0:T(8,128)S(1)}, f32[4,64,128]{2,1,0:T(8,128)S(1)}, u32[]{:S(2)}, u32[]{:S(2)}) collective-permute-start(f32[4,64,128]{2,1,0:T(8,128)S(1)} %get-tuple-element.93), channel_id=1, source_target_pairs={{0,1},{1,2},{2,3},{3,4},{4,5},{5,6},{6,7},{7,8},{8,9},{9,10},{10,1... | collective-permute-start | bytes 393224 | tf_op jit(solution)/shard_map/ppermute | solution.py:24
  314.6 1.9 collective-permute-start.24
  316.6 2.5 collective-permute-done.24
  319.0 2.1 multiply_subtract_fusion.3
  321.3 9.8 %collective-permute-start.27 = (f32[4,64,128]{2,1,0:T(8,128)S(1)}, f32[4,64,128]{2,1,0:T(8,128)S(1)}, u32[]{:S(2)}, u32[]{:S(2)}) collective-permute-start(f32[4,64,128]{2,1,0:T(8,128)S(1)} %get-tuple-element.91), channel_id=1, source_target_pairs={{0,1},{1,2},{2,3},{3,4},{4,5},{5,6},{6,7},{7,8},{8,9},{9,10},{10,1... | collective-permute-start | bytes 393224 | tf_op jit(solution)/shard_map/ppermute | solution.py:24
  331.1 1.9 collective-permute-start.26
  333.0 2.5 collective-permute-done.26
  335.5 1.3 select_add_fusion
  336.8 9.8 %collective-permute-start.29 = (f32[4,64,128]{2,1,0:T(8,128)S(1)}, f32[4,64,128]{2,1,0:T(8,128)S(1)}, u32[]{:S(2)}, u32[]{:S(2)}) collective-permute-start(f32[4,64,128]{2,1,0:T(8,128)S(1)} %get-tuple-element.89), channel_id=1, source_target_pairs={{0,1},{1,2},{2,3},{3,4},{4,5},{5,6},{6,7},{7,8},{8,9},{9,10},{10,1... | collective-permute-start | bytes 393224 | tf_op jit(solution)/shard_map/ppermute | solution.py:24
  346.6 1.9 collective-permute-start.28
  348.6 2.4 collective-permute-start.11
  351.0 3.2 collective-permute-start.10
  354.2 2.1 multiply_subtract_fusion
  356.4 7.9 %collective-permute-start.31 = (f32[4,64,128]{2,1,0:T(8,128)S(1)}, f32[4,64,128]{2,1,0:T(8,128)S(1)}, u32[]{:S(2)}, u32[]{:S(2)}) collective-permute-start(f32[4,64,128]{2,1,0:T(8,128)S(1)} %get-tuple-element.87), channel_id=1, source_target_pairs={{0,1},{1,2},{2,3},{3,4},{4,5},{5,6},{6,7},{7,8},{8,9},{9,10},{10,1... | collective-permute-start | bytes 393224 | tf_op jit(solution)/shard_map/ppermute | solution.py:24
  364.4 1.9 collective-permute-start.30
  366.7 8.2 %collective-permute-done.30 = f32[4,64,128]{2,1,0:T(8,128)S(1)} collective-permute-done((f32[4,64,128]{2,1,0:T(8,128)S(1)}, f32[4,64,128]{2,1,0:T(8,128)S(1)}, u32[]{:S(2)}, u32[]{:S(2)}) %collective-permute-start.30) | collective-permute-done | bytes 131104 | tf_op jit(solution)/shard_map/ppermute | solution.py:25
  374.9 2.1 fusion.198
  377.8 11.5 %collective-permute-start.13 = (f32[4,64,128]{2,1,0:T(8,128)}, f32[4,64,128]{2,1,0:T(8,128)S(1)}, u32[]{:S(2)}, u32[]{:S(2)}) collective-permute-start(f32[4,64,128]{2,1,0:T(8,128)} %get-tuple-element.73), channel_id=1, source_target_pairs={{0,1},{1,2},{2,3},{3,4},{4,5},{5,6},{6,7},{7,8},{8,9},{9,10},{10,1... | collective-permute-start | bytes 393224 | tf_op jit(solution)/shard_map/ppermute | solution.py:24
  389.2 1.9 collective-permute-start.12
  392.0 1.7 dynamic_update_slice.19
  394.0 2.9 multiply_subtract_fusion.12
  397.1 9.8 %collective-permute-start.15 = (f32[4,64,128]{2,1,0:T(8,128)S(1)}, f32[4,64,128]{2,1,0:T(8,128)S(1)}, u32[]{:S(2)}, u32[]{:S(2)}) collective-permute-start(f32[4,64,128]{2,1,0:T(8,128)S(1)} %get-tuple-element.71), channel_id=1, source_target_pairs={{0,1},{1,2},{2,3},{3,4},{4,5},{5,6},{6,7},{7,8},{8,9},{9,10},{10,1... | collective-permute-start | bytes 393224 | tf_op jit(solution)/shard_map/ppermute | solution.py:24
  406.9 1.9 collective-permute-start.14
  409.2 2.1 collective-permute-done.14
  411.3 1.3 fusion.98
  412.7 67.0 %reduce-scatter.2.cloned.1.call-done = f32[8,8,128]{2,1,0:T(8,128)} async-done(((f32[8,128,128]{2,1,0:T(8,128)}), f32[8,8,128]{2,1,0:T(8,128)}) %reduce-scatter.2.cloned.1.call-update) | async-done | bytes 32784 | tf_op jit(solution)/shard_map/reduce_scatter | solution.py:164
  (119 shorter events, 15.2 us)
Async XLA Ops:
  7.2 11.6 %copy-start.4 = (f32[1,8,64,128]{3,2,1,0:T(8,128)S(1)}, f32[1,8,64,128]{3,2,1,0:T(8,128)}, u32[]{:S(2)}) copy-start(f32[1,8,64,128]{3,2,1,0:T(8,128)} %param.19) | copy-start | bytes 786436
  7.2 18.5 %copy-start.13 = (f32[8,8,128]{2,1,0:T(8,128)S(1)}, f32[8,8,128]{2,1,0:T(8,128)}, u32[]{:S(2)}) copy-start(f32[8,8,128]{2,1,0:T(8,128)} %param.22) | copy-start | bytes 98308
  8.8 176.8 %all-to-all-start = ((f32[16,8,8,128]{3,2,1,0:T(8,128)}), f32[16,8,8,128]{3,2,1,0:T(8,128)S(1)}, u32[]{:S(2)}, u32[]{:S(2)}) async-start(f32[16,8,8,128]{3,2,1,0:T(8,128)} %stack.2), calls=%async_computation | async-start | bytes 1048576 | tf_op jit(solution)/shard_map/all_to_all | solution.py:13
  18.7 461.1 %reduce-scatter.2.cloned.1.call-start = ((), (), s32[]{:S(2)}) async-start(), calls=%async_computation.2 | async-start | bytes 557056 | tf_op jit(solution)/shard_map/reduce_scatter | solution.py:164
  19.5 169.9 %collective-permute-start.17 = (f32[4,64,128]{2,1,0:T(8,128)}, f32[4,64,128]{2,1,0:T(8,128)}, u32[]{:S(2)}, u32[]{:S(2)}) collective-permute-start(f32[4,64,128]{2,1,0:T(8,128)} %get-tuple-element.101), channel_id=1, source_target_pairs={{0,1},{1,2},{2,3},{3,4},{4,5},{5,6},{6,7},{7,8},{8,9},{9,10},{10,1... | collective-permute-start | bytes 393224 | tf_op jit(solution)/shard_map/ppermute | solution.py:24
  21.4 168.0 %collective-permute-start.16 = (f32[4,64,128]{2,1,0:T(8,128)}, f32[4,64,128]{2,1,0:T(8,128)}, u32[]{:S(2)}, u32[]{:S(2)}) collective-permute-start(f32[4,64,128]{2,1,0:T(8,128)} %get-tuple-element.100), channel_id=1, source_target_pairs={{1,0},{2,1},{3,2},{4,3},{5,4},{6,5},{7,6},{8,7},{9,8},{10,9},{11,1... | collective-permute-start | bytes 393224 | tf_op jit(solution)/shard_map/ppermute | solution.py:25
  75.0 1.6 copy-start.5
  75.1 9.3 %copy-start.23 = (s32[1,128]{1,0:T(1,128)S(1)}, s32[1,128]{1,0:T(1,128)}, u32[]{:S(2)}) copy-start(s32[1,128]{1,0:T(1,128)} %param.33) | copy-start | bytes 1540
  75.1 9.3 %copy-start.22 = (s32[1,128]{1,0:T(1,128)S(1)}, s32[1,128]{1,0:T(1,128)}, u32[]{:S(2)}) copy-start(s32[1,128]{1,0:T(1,128)} %param.34) | copy-start | bytes 1540
  75.1 10.7 %copy-start.16 = (s32[1,128]{1,0:T(1,128)S(1)}, s32[1,128]{1,0:T(1,128)}, u32[]{:S(2)}) copy-start(s32[1,128]{1,0:T(1,128)} %param.35) | copy-start | bytes 1540
  75.1 13.5 %copy-start.14 = (f32[8,8,128]{2,1,0:T(8,128)S(1)}, f32[8,8,128]{2,1,0:T(8,128)}, u32[]{:S(2)}) copy-start(f32[8,8,128]{2,1,0:T(8,128)} %param.23) | copy-start | bytes 98308
  76.6 99.0 %copy-start.2 = (f32[8,320,128]{2,1,0:T(8,128)}, f32[8,320,128]{2,1,0:T(8,128)S(1)}, u32[]{:S(2)}) copy-start(f32[8,320,128]{2,1,0:T(8,128)S(1)} %dynamic_update_slice.16) | copy-start | bytes 3932164
  76.6 56.1 %copy-start.15 = (f32[8,8,128]{2,1,0:T(8,128)S(1)}, f32[8,8,128]{2,1,0:T(8,128)}, u32[]{:S(2)}) copy-start(f32[8,8,128]{2,1,0:T(8,128)} %param.25) | copy-start | bytes 98308
  77.5 117.3 %collective-permute-start.1 = (f32[4,64,128]{2,1,0:T(8,128)}, f32[4,64,128]{2,1,0:T(8,128)S(1)}, u32[]{:S(2)}, u32[]{:S(2)}) collective-permute-start(f32[4,64,128]{2,1,0:T(8,128)} %get-tuple-element.85), channel_id=1, source_target_pairs={{0,1},{1,2},{2,3},{3,4},{4,5},{5,6},{6,7},{7,8},{8,9},{9,10},{10,1... | collective-permute-start | bytes 393224 | tf_op jit(solution)/shard_map/ppermute | solution.py:24
  79.4 115.4 %collective-permute-start = (f32[4,64,128]{2,1,0:T(8,128)}, f32[4,64,128]{2,1,0:T(8,128)}, u32[]{:S(2)}, u32[]{:S(2)}) collective-permute-start(f32[4,64,128]{2,1,0:T(8,128)} %get-tuple-element.84), channel_id=1, source_target_pairs={{1,0},{2,1},{3,2},{4,3},{5,4},{6,5},{7,6},{8,7},{9,8},{10,9},{11,1... | collective-permute-start | bytes 393224 | tf_op jit(solution)/shard_map/ppermute | solution.py:25
  179.7 4.7 copy-start.19
  189.3 1.1 copy-start
  194.7 1.3 copy-start.1
  198.1 25.9 %copy-start.3 = (f32[8,320,128]{2,1,0:T(8,128)S(1)}, f32[8,320,128]{2,1,0:T(8,128)}, u32[]{:S(2)}) copy-start(f32[8,320,128]{2,1,0:T(8,128)} %copy-done.2) | copy-start | bytes 3932164
  198.1 25.9 %copy-start.10 = (f32[512,128]{1,0:T(8,128)S(1)}, f32[512,128]{1,0:T(8,128)}, u32[]{:S(2)}) copy-start(f32[512,128]{1,0:T(8,128)} %fusion.663) | copy-start | bytes 786436
  198.1 25.9 %copy-start.12 = (f32[1,8,64,128]{3,2,1,0:T(8,128)S(1)}, f32[1,8,64,128]{3,2,1,0:T(8,128)}, u32[]{:S(2)}) copy-start(f32[1,8,64,128]{3,2,1,0:T(8,128)} %param.20) | copy-start | bytes 786436
  198.3 25.7 %collective-permute-start.3 = (f32[4,64,128]{2,1,0:T(8,128)S(1)}, f32[4,64,128]{2,1,0:T(8,128)S(1)}, u32[]{:S(2)}, u32[]{:S(2)}) collective-permute-start(f32[4,64,128]{2,1,0:T(8,128)S(1)} %get-tuple-element.83), channel_id=1, source_target_pairs={{0,1},{1,2},{2,3},{3,4},{4,5},{5,6},{6,7},{7,8},{8,9},{9,10},{10,1... | collective-permute-start | bytes 393224 | tf_op jit(solution)/shard_map/ppermute | solution.py:24
  200.4 23.7 %collective-permute-start.2 = (f32[4,64,128]{2,1,0:T(8,128)S(1)}, f32[4,64,128]{2,1,0:T(8,128)S(1)}, u32[]{:S(2)}, u32[]{:S(2)}) collective-permute-start(f32[4,64,128]{2,1,0:T(8,128)S(1)} %get-tuple-element.82), channel_id=1, source_target_pairs={{1,0},{2,1},{3,2},{4,3},{5,4},{6,5},{7,6},{8,7},{9,8},{10,9},{11,1... | collective-permute-start | bytes 393224 | tf_op jit(solution)/shard_map/ppermute | solution.py:25
  204.1 32.3 %collective-permute-start.19 = (f32[4,64,128]{2,1,0:T(8,128)S(1)}, f32[4,64,128]{2,1,0:T(8,128)S(1)}, u32[]{:S(2)}, u32[]{:S(2)}) collective-permute-start(f32[4,64,128]{2,1,0:T(8,128)S(1)} %get-tuple-element.99), channel_id=1, source_target_pairs={{0,1},{1,2},{2,3},{3,4},{4,5},{5,6},{6,7},{7,8},{8,9},{9,10},{10,1... | collective-permute-start | bytes 393224 | tf_op jit(solution)/shard_map/ppermute | solution.py:24
  222.1 14.3 %collective-permute-start.18 = (f32[4,64,128]{2,1,0:T(8,128)S(1)}, f32[4,64,128]{2,1,0:T(8,128)S(1)}, u32[]{:S(2)}, u32[]{:S(2)}) collective-permute-start(f32[4,64,128]{2,1,0:T(8,128)S(1)} %get-tuple-element.98), channel_id=1, source_target_pairs={{1,0},{2,1},{3,2},{4,3},{5,4},{6,5},{7,6},{8,7},{9,8},{10,9},{11,1... | collective-permute-start | bytes 393224 | tf_op jit(solution)/shard_map/ppermute | solution.py:25
  224.1 12.3 %copy-start.11 = (f32[1,8,64,128]{3,2,1,0:T(8,128)S(1)}, f32[1,8,64,128]{3,2,1,0:T(8,128)}, u32[]{:S(2)}) copy-start(f32[1,8,64,128]{3,2,1,0:T(8,128)} %param.18) | copy-start | bytes 786436
  224.1 12.3 %copy-start.17 = (pred[64]{0:T(512)(128)(4,1)S(1)}, pred[64]{0:T(512)(128)(4,1)}, u32[]{:S(2)}) copy-start(pred[64]{0:T(512)(128)(4,1)} %iota_compare_fusion.7) | copy-start | bytes 196
  224.1 12.3 %copy-start.18 = (pred[8]{0:T(512)(128)(4,1)S(1)}, pred[8]{0:T(512)(128)(4,1)}, u32[]{:S(2)}) copy-start(pred[8]{0:T(512)(128)(4,1)} %add_compare_fusion) | copy-start | bytes 28
  224.8 13.0 %collective-permute-start.5 = (f32[4,64,128]{2,1,0:T(8,128)S(1)}, f32[4,64,128]{2,1,0:T(8,128)S(1)}, u32[]{:S(2)}, u32[]{:S(2)}) collective-permute-start(f32[4,64,128]{2,1,0:T(8,128)S(1)} %get-tuple-element.81), channel_id=1, source_target_pairs={{0,1},{1,2},{2,3},{3,4},{4,5},{5,6},{6,7},{7,8},{8,9},{9,10},{10,1... | collective-permute-start | bytes 393224 | tf_op jit(solution)/shard_map/ppermute | solution.py:24
  234.4 10.5 %collective-permute-start.4 = (f32[4,64,128]{2,1,0:T(8,128)S(1)}, f32[4,64,128]{2,1,0:T(8,128)S(1)}, u32[]{:S(2)}, u32[]{:S(2)}) collective-permute-start(f32[4,64,128]{2,1,0:T(8,128)S(1)} %get-tuple-element.80), channel_id=1, source_target_pairs={{1,0},{2,1},{3,2},{4,3},{5,4},{6,5},{7,6},{8,7},{9,8},{10,9},{11,1... | collective-permute-start | bytes 393224 | tf_op jit(solution)/shard_map/ppermute | solution.py:25
  247.0 19.2 %copy-start.9 = (f32[512,128]{1,0:T(8,128)S(1)}, f32[512,128]{1,0:T(8,128)}, u32[]{:S(2)}) copy-start(f32[512,128]{1,0:T(8,128)} %fusion.661) | copy-start | bytes 786436
  247.2 19.0 %collective-permute-start.7 = (f32[4,64,128]{2,1,0:T(8,128)S(1)}, f32[4,64,128]{2,1,0:T(8,128)S(1)}, u32[]{:S(2)}, u32[]{:S(2)}) collective-permute-start(f32[4,64,128]{2,1,0:T(8,128)S(1)} %get-tuple-element.79), channel_id=1, source_target_pairs={{0,1},{1,2},{2,3},{3,4},{4,5},{5,6},{6,7},{7,8},{8,9},{9,10},{10,1... | collective-permute-start | bytes 393224 | tf_op jit(solution)/shard_map/ppermute | solution.py:24
  258.6 7.5 %collective-permute-start.6 = (f32[4,64,128]{2,1,0:T(8,128)S(1)}, f32[4,64,128]{2,1,0:T(8,128)S(1)}, u32[]{:S(2)}, u32[]{:S(2)}) collective-permute-start(f32[4,64,128]{2,1,0:T(8,128)S(1)} %get-tuple-element.78), channel_id=1, source_target_pairs={{1,0},{2,1},{3,2},{4,3},{5,4},{6,5},{7,6},{8,7},{9,8},{10,9},{11,1... | collective-permute-start | bytes 393224 | tf_op jit(solution)/shard_map/ppermute | solution.py:25
  260.6 16.3 %collective-permute-start.21 = (f32[4,64,128]{2,1,0:T(8,128)S(1)}, f32[4,64,128]{2,1,0:T(8,128)S(1)}, u32[]{:S(2)}, u32[]{:S(2)}) collective-permute-start(f32[4,64,128]{2,1,0:T(8,128)S(1)} %get-tuple-element.97), channel_id=1, source_target_pairs={{0,1},{1,2},{2,3},{3,4},{4,5},{5,6},{6,7},{7,8},{8,9},{9,10},{10,1... | collective-permute-start | bytes 393224 | tf_op jit(solution)/shard_map/ppermute | solution.py:24
  263.0 13.9 %collective-permute-start.20 = (f32[4,64,128]{2,1,0:T(8,128)S(1)}, f32[4,64,128]{2,1,0:T(8,128)S(1)}, u32[]{:S(2)}, u32[]{:S(2)}) collective-permute-start(f32[4,64,128]{2,1,0:T(8,128)S(1)} %get-tuple-element.96), channel_id=1, source_target_pairs={{1,0},{2,1},{3,2},{4,3},{5,4},{6,5},{7,6},{8,7},{9,8},{10,9},{11,1... | collective-permute-start | bytes 393224 | tf_op jit(solution)/shard_map/ppermute | solution.py:25
  266.9 108.0 %copy-start.7 = (f32[8,64,128]{2,1,0:T(8,128)}, f32[8,64,128]{2,1,0:T(8,128)S(1)}, u32[]{:S(2)}) copy-start(f32[8,64,128]{2,1,0:T(8,128)S(1)} %get-tuple-element.43) | copy-start | bytes 786436
  266.9 12.2 %collective-permute-start.9 = (f32[4,64,128]{2,1,0:T(8,128)S(1)}, f32[4,64,128]{2,1,0:T(8,128)S(1)}, u32[]{:S(2)}, u32[]{:S(2)}) collective-permute-start(f32[4,64,128]{2,1,0:T(8,128)S(1)} %get-tuple-element.77), channel_id=1, source_target_pairs={{0,1},{1,2},{2,3},{3,4},{4,5},{5,6},{6,7},{7,8},{8,9},{9,10},{10,1... | collective-permute-start | bytes 393224 | tf_op jit(solution)/shard_map/ppermute | solution.py:24
  274.8 10.5 %collective-permute-start.8 = (f32[4,64,128]{2,1,0:T(8,128)S(1)}, f32[4,64,128]{2,1,0:T(8,128)S(1)}, u32[]{:S(2)}, u32[]{:S(2)}) collective-permute-start(f32[4,64,128]{2,1,0:T(8,128)S(1)} %get-tuple-element.76), channel_id=1, source_target_pairs={{1,0},{2,1},{3,2},{4,3},{5,4},{6,5},{7,6},{8,7},{9,8},{10,9},{11,1... | collective-permute-start | bytes 393224 | tf_op jit(solution)/shard_map/ppermute | solution.py:25
  287.6 13.4 %collective-permute-start.23 = (f32[4,64,128]{2,1,0:T(8,128)S(1)}, f32[4,64,128]{2,1,0:T(8,128)S(1)}, u32[]{:S(2)}, u32[]{:S(2)}) collective-permute-start(f32[4,64,128]{2,1,0:T(8,128)S(1)} %get-tuple-element.95), channel_id=1, source_target_pairs={{0,1},{1,2},{2,3},{3,4},{4,5},{5,6},{6,7},{7,8},{8,9},{9,10},{10,1... | collective-permute-start | bytes 393224 | tf_op jit(solution)/shard_map/ppermute | solution.py:24
  299.1 4.4 collective-permute-start.22
  304.8 11.7 %collective-permute-start.25 = (f32[4,64,128]{2,1,0:T(8,128)S(1)}, f32[4,64,128]{2,1,0:T(8,128)S(1)}, u32[]{:S(2)}, u32[]{:S(2)}) collective-permute-start(f32[4,64,128]{2,1,0:T(8,128)S(1)} %get-tuple-element.93), channel_id=1, source_target_pairs={{0,1},{1,2},{2,3},{3,4},{4,5},{5,6},{6,7},{7,8},{8,9},{9,10},{10,1... | collective-permute-start | bytes 393224 | tf_op jit(solution)/shard_map/ppermute | solution.py:24
  314.6 4.4 collective-permute-start.24
  321.3 11.7 %collective-permute-start.27 = (f32[4,64,128]{2,1,0:T(8,128)S(1)}, f32[4,64,128]{2,1,0:T(8,128)S(1)}, u32[]{:S(2)}, u32[]{:S(2)}) collective-permute-start(f32[4,64,128]{2,1,0:T(8,128)S(1)} %get-tuple-element.91), channel_id=1, source_target_pairs={{0,1},{1,2},{2,3},{3,4},{4,5},{5,6},{6,7},{7,8},{8,9},{9,10},{10,1... | collective-permute-start | bytes 393224 | tf_op jit(solution)/shard_map/ppermute | solution.py:24
  331.1 4.4 collective-permute-start.26
  336.8 17.3 %collective-permute-start.29 = (f32[4,64,128]{2,1,0:T(8,128)S(1)}, f32[4,64,128]{2,1,0:T(8,128)S(1)}, u32[]{:S(2)}, u32[]{:S(2)}) collective-permute-start(f32[4,64,128]{2,1,0:T(8,128)S(1)} %get-tuple-element.89), channel_id=1, source_target_pairs={{0,1},{1,2},{2,3},{3,4},{4,5},{5,6},{6,7},{7,8},{8,9},{9,10},{10,1... | collective-permute-start | bytes 393224 | tf_op jit(solution)/shard_map/ppermute | solution.py:24
  346.6 7.5 %collective-permute-start.28 = (f32[4,64,128]{2,1,0:T(8,128)S(1)}, f32[4,64,128]{2,1,0:T(8,128)S(1)}, u32[]{:S(2)}, u32[]{:S(2)}) collective-permute-start(f32[4,64,128]{2,1,0:T(8,128)S(1)} %get-tuple-element.88), channel_id=1, source_target_pairs={{1,0},{2,1},{3,2},{4,3},{5,4},{6,5},{7,6},{8,7},{9,8},{10,9},{11,1... | collective-permute-start | bytes 393224 | tf_op jit(solution)/shard_map/ppermute | solution.py:25
  348.6 18.1 %collective-permute-start.11 = (f32[4,64,128]{2,1,0:T(8,128)S(1)}, f32[4,64,128]{2,1,0:T(8,128)S(1)}, u32[]{:S(2)}, u32[]{:S(2)}) collective-permute-start(f32[4,64,128]{2,1,0:T(8,128)S(1)} %get-tuple-element.75), channel_id=1, source_target_pairs={{0,1},{1,2},{2,3},{3,4},{4,5},{5,6},{6,7},{7,8},{8,9},{9,10},{10,1... | collective-permute-start | bytes 393224 | tf_op jit(solution)/shard_map/ppermute | solution.py:24
  351.0 15.7 %collective-permute-start.10 = (f32[4,64,128]{2,1,0:T(8,128)S(1)}, f32[4,64,128]{2,1,0:T(8,128)S(1)}, u32[]{:S(2)}, u32[]{:S(2)}) collective-permute-start(f32[4,64,128]{2,1,0:T(8,128)S(1)} %get-tuple-element.74), channel_id=1, source_target_pairs={{1,0},{2,1},{3,2},{4,3},{5,4},{6,5},{7,6},{8,7},{9,8},{10,9},{11,1... | collective-permute-start | bytes 393224 | tf_op jit(solution)/shard_map/ppermute | solution.py:25
  356.3 10.1 %copy-start.21 = (f32[128]{0:T(128)S(1)}, f32[128]{0:T(128)}, u32[]{:S(2)}) copy-start(f32[128]{0:T(128)} %get-tuple-element.105) | copy-start | bytes 1540
  356.4 10.3 %collective-permute-start.31 = (f32[4,64,128]{2,1,0:T(8,128)S(1)}, f32[4,64,128]{2,1,0:T(8,128)S(1)}, u32[]{:S(2)}, u32[]{:S(2)}) collective-permute-start(f32[4,64,128]{2,1,0:T(8,128)S(1)} %get-tuple-element.87), channel_id=1, source_target_pairs={{0,1},{1,2},{2,3},{3,4},{4,5},{5,6},{6,7},{7,8},{8,9},{9,10},{10,1... | collective-permute-start | bytes 393224 | tf_op jit(solution)/shard_map/ppermute | solution.py:24
  364.4 10.5 %collective-permute-start.30 = (f32[4,64,128]{2,1,0:T(8,128)S(1)}, f32[4,64,128]{2,1,0:T(8,128)S(1)}, u32[]{:S(2)}, u32[]{:S(2)}) collective-permute-start(f32[4,64,128]{2,1,0:T(8,128)S(1)} %get-tuple-element.86), channel_id=1, source_target_pairs={{1,0},{2,1},{3,2},{4,3},{5,4},{6,5},{7,6},{8,7},{9,8},{10,9},{11,1... | collective-permute-start | bytes 393224 | tf_op jit(solution)/shard_map/ppermute | solution.py:25
  377.0 34.3 %copy-start.6 = (f32[8,64,128]{2,1,0:T(8,128)}, f32[8,64,128]{2,1,0:T(8,128)S(1)}, u32[]{:S(2)}) copy-start(f32[8,64,128]{2,1,0:T(8,128)S(1)} %get-tuple-element.4) | copy-start | bytes 786436
  377.8 16.0 %collective-permute-start.13 = (f32[4,64,128]{2,1,0:T(8,128)}, f32[4,64,128]{2,1,0:T(8,128)S(1)}, u32[]{:S(2)}, u32[]{:S(2)}) collective-permute-start(f32[4,64,128]{2,1,0:T(8,128)} %get-tuple-element.73), channel_id=1, source_target_pairs={{0,1},{1,2},{2,3},{3,4},{4,5},{5,6},{6,7},{7,8},{8,9},{9,10},{10,1... | collective-permute-start | bytes 393224 | tf_op jit(solution)/shard_map/ppermute | solution.py:24
  389.2 4.7 collective-permute-start.12
  396.9 11.9 %copy-start.20 = (f32[128]{0:T(128)S(1)}, f32[128]{0:T(128)}, u32[]{:S(2)}) copy-start(f32[128]{0:T(128)} %get-tuple-element.102) | copy-start | bytes 1540
  396.9 14.4 %copy-start.8 = (f32[8,64,128]{2,1,0:T(8,128)S(1)}, f32[8,64,128]{2,1,0:T(8,128)}, u32[]{:S(2)}) copy-start(f32[8,64,128]{2,1,0:T(8,128)} %copy-done.7) | copy-start | bytes 786436
  397.1 12.1 %collective-permute-start.15 = (f32[4,64,128]{2,1,0:T(8,128)S(1)}, f32[4,64,128]{2,1,0:T(8,128)S(1)}, u32[]{:S(2)}, u32[]{:S(2)}) collective-permute-start(f32[4,64,128]{2,1,0:T(8,128)S(1)} %get-tuple-element.71), channel_id=1, source_target_pairs={{0,1},{1,2},{2,3},{3,4},{4,5},{5,6},{6,7},{7,8},{8,9},{9,10},{10,1... | collective-permute-start | bytes 393224 | tf_op jit(solution)/shard_map/ppermute | solution.py:24
  406.9 4.4 collective-permute-start.14
Sparse Core Ops, SparseCore 0:
  393.9 85.7 reduce-scatter.1
